TPU v7x, 256 devices: a whole 4x4x8 slice. The times are simulated.
256 devices in a mesh: dom: 32 (over y, z), feat: 8 (over x, core).
Axes of the slice: x: 4, y: 4, z: 8, core: 2. Of those that a mesh axis runs over, the one named last changes fastest.
Arguments:
- feats: bfloat16 [131072, 1024], P('dom', 'feat'), may hold values from -6 to 6
- projection: bfloat16 [1024, 512], P('feat'), may hold values from -0.1875 to 0.1875
- tiles: bfloat16 [8192, 4, 128, 128], P(('dom', 'feat')), may hold values from -0.25 to 0.25
- slot_owner: int32 [8192, 1], P(('dom', 'feat')), may hold values from 0 to 31; in each aligned block of 32 rows (0 to 31, 32 to 63, ...) at most 2 rows name the same one
- slot_block: int32 [8192, 1], P(('dom', 'feat')), may hold values from 0 to 3
- source_block: int32 [8192, 4], P(('dom', 'feat')), may hold values from 0 to 3
- counts: int32 [131072], P(('dom', 'feat')), may hold values from 1 to 4
- out_grad: bfloat16 [131072, 256], P(('dom', 'feat')), may hold values from -0.015625 to 0.015625
Outputs:
- activated: bfloat16 [131072, 256], P(('dom', 'feat'))
- weight_grad: float32 [1024, 512], P('feat')
Inputs may be any that keep to these rules, and one draw needn't show every extreme that they name: `slot_owner`: among the 32 sent rows of one device, no dom index is named more than 2 times; some device names one exactly 2 times.
All inputs are finite; a program needn't handle non-finite values.
Results may differ from a plain program's by a relative error of at most 0.0059.
Values may be sent and summed in bfloat16 or wider, within the bound.
A program may use at most 128 MiB of HBM per device.

v0:
```python
import jax
import jax.numpy as jnp
from jax import lax
from jax.sharding import PartitionSpec as P


def local(feats, projection, tiles, slot_owner, slot_block, source_block, counts, out_grad):
    tile_size = tiles.shape[-1]
    slot_count = tiles.shape[0]
    per_slot = tiles.shape[1]
    out_width = out_grad.shape[1]
    node_rows = out_grad.shape[0]
    block_count = node_rows // tile_size
    dom_count = lax.axis_size("dom")
    capacity = max(2, 2 * slot_count // dom_count)
    flat_width = tile_size * out_width
    projected = lax.psum_scatter(
        jnp.dot(feats, projection, preferred_element_type=jnp.float32),
        "feat",
        scatter_dimension=0,
        tiled=True,
    ).astype(jnp.bfloat16)
    neighbour = projected[:, :out_width].reshape(block_count, tile_size, out_width)
    self_part = projected[:, out_width:]
    picked = neighbour[source_block]
    contribution = jnp.einsum("skij,skjh->sih", tiles, picked, preferred_element_type=jnp.float32)
    contribution = contribution.astype(jnp.bfloat16).reshape(slot_count, flat_width)
    slot_dest = slot_owner[:, 0]
    dest_block = slot_block[:, 0]
    dest_hot = (slot_dest[:, None] == jnp.arange(dom_count, dtype=jnp.int32)[None, :]).astype(
        jnp.int32
    )
    before = jnp.cumsum(dest_hot, axis=0) - dest_hot
    position = jnp.sum(before * dest_hot, axis=1)
    slot_index = slot_dest * capacity + position
    placing = jnp.arange(dom_count * capacity, dtype=jnp.int32)[:, None] == slot_index[None, :]
    outgoing = jnp.dot(
        placing.astype(jnp.bfloat16), contribution, preferred_element_type=jnp.float32
    )
    outgoing = outgoing.astype(jnp.bfloat16).reshape(dom_count, capacity, flat_width)
    labels = jnp.sum(placing.astype(jnp.int32) * (dest_block + 1)[None, :], axis=1) - 1
    labels = labels.reshape(dom_count, capacity)
    incoming, got_labels = (
        lax.all_to_all(outgoing, "dom", split_axis=0, concat_axis=0, tiled=True),
        lax.all_to_all(labels, "dom", split_axis=0, concat_axis=0, tiled=True),
    )
    incoming = incoming.reshape(dom_count * capacity, flat_width)
    receive_hot = (
        jnp.arange(block_count, dtype=jnp.int32)[:, None] == got_labels.reshape(-1)[None, :]
    ).astype(jnp.bfloat16)
    summed = jnp.dot(receive_hot, incoming, preferred_element_type=jnp.float32).reshape(
        node_rows, out_width
    )
    degree = counts.astype(jnp.float32)[:, None]
    preact = summed / degree + self_part.astype(jnp.float32)
    sigma = jax.nn.sigmoid(preact)
    activated = (preact * sigma).astype(jnp.bfloat16)
    grad_pre = out_grad.astype(jnp.float32) * sigma * (1.0 + preact * (1.0 - sigma))
    grad_self = grad_pre.astype(jnp.bfloat16)
    grad_sum = (grad_pre / degree).astype(jnp.bfloat16).reshape(block_count, flat_width)
    sending_back = jnp.dot(receive_hot.T, grad_sum, preferred_element_type=jnp.float32)
    sending_back = sending_back.astype(jnp.bfloat16).reshape(dom_count, capacity, flat_width)
    returned = lax.all_to_all(sending_back, "dom", split_axis=0, concat_axis=0, tiled=True).reshape(
        dom_count * capacity, flat_width
    )
    slot_grad = jnp.dot(
        placing.T.astype(jnp.bfloat16), returned, preferred_element_type=jnp.float32
    )
    slot_grad = slot_grad.astype(jnp.bfloat16).reshape(slot_count, tile_size, out_width)
    products = jnp.einsum("skij,sih->skjh", tiles, slot_grad, preferred_element_type=jnp.float32)
    source_hot = (
        jnp.arange(block_count, dtype=jnp.int32)[:, None] == source_block.reshape(-1)[None, :]
    ).astype(jnp.float32)
    flat_products = products.reshape(slot_count * per_slot, tile_size, out_width)
    grad_neigh = jnp.einsum(
        "bn,njh->bjh", source_hot, flat_products, precision=lax.Precision.HIGHEST
    )
    grad_neigh = grad_neigh.astype(jnp.bfloat16).reshape(node_rows, out_width)
    grad_proj = jnp.concatenate([grad_neigh, grad_self], axis=1)
    partial_grad = lax.dot_general(
        feats,
        lax.all_gather(grad_proj, "feat", axis=0, tiled=True),
        (((0,), (0,)), ((), ())),
        preferred_element_type=jnp.float32,
    )
    weight_grad = lax.psum(partial_grad, "dom")
    return (activated, weight_grad)


def solution(mesh):
    placed = (
        P("dom", "feat"),
        P("feat", None),
        P(("dom", "feat"), None, None, None),
        P(("dom", "feat"), None),
        P(("dom", "feat"), None),
        P(("dom", "feat"), None),
        P(("dom", "feat")),
        P(("dom", "feat"), None),
    )
    return jax.shard_map(
        local,
        mesh=mesh,
        in_specs=placed,
        out_specs=(P(("dom", "feat"), None), P("feat", None)),
        check_vma=False,
    )
```

profile of v0, /device:TPU:2, one launch (start us, length us, event | category | flops | bytes accessed | tf_op | source)
XLA Modules:
  0.0 570.8 jit_solution(17779581834681642743)
XLA Ops:
  7.2 1.2 copy-done
  8.4 5.4 fusion.12
  13.8 0.6 copy-done.6
  14.4 0.1 fusion.3
  14.5 0.1 reduce_window_sum.11
  14.6 0.2 select_reduce_fusion.1
  14.8 0.1 select_reduce_fusion
  14.9 0.7 sub.14
  15.6 11.5 %all-to-all-start = ((s32[32,1,2]{2,1,0:T(1,128)}), s32[32,1,2]{2,1,0:T(1,128)S(1)}, u32[]{:S(2)}, u32[]{:S(2)}) async-start(s32[32,1,2]{2,1,0:T(1,128)} %bitcast.2), calls=%async_computation | async-start | bytes 32768 | tf_op jit(solution)/shard_map/all_to_all | solution.py:45
  27.1 0.1 copy.35
  27.2 0.1 reshape.85
  27.3 42.2 %reduce-scatter.2.cloned.1.call-done = f32[512,512]{1,0:T(8,128)} async-done(((f32[4096,512]{1,0:T(8,128)}), f32[512,512]{1,0:T(8,128)}) %reduce-scatter.2.cloned.1.call-update) | async-done | bytes 1048592 | tf_op jit(solution)/shard_map/reduce_scatter | solution.py:17
  69.5 1.3 convert_element_type.48
  70.8 0.8 copy-done.2
  71.7 6.5 %gather_fusion = bf16[128,128,256]{2,1,0:T(8,128)(2,1)} fusion(bf16[4,128,256]{2,1,0:T(8,128)(2,1)S(1)} %bitcast.46, s32[1024]{0:T(1024)S(1)} %pad_clamp_fusion), kind=kCustom, calls=%fused_computation | custom fusion | bytes 16777728 | tf_op jit(solution)/shard_map/gather | solution.py:25
  78.2 7.0 %fusion.2 = bf16[32,128,256]{1,2,0:T(8,128)(2,1)S(1)} fusion(bf16[32,4,128,256]{3,2,1,0:T(8,128)(2,1)} %bitcast.48, bf16[32,4,128,128]{3,2,1,0:T(8,128)(2,1)} %param.10), kind=kOutput, calls=%fused_computation.7 | convolution fusion | flops 1074790400 | bytes 14680064 | tf_op jit(solution)/shard_map/skij,skjh->sih/dot_general | solution.py:26
  85.2 2.9 copy.47
  88.1 4.9 convolution_convert_fusion.1
  93.0 7.6 %reshape.74 = bf16[32,2,32768]{2,1,0:T(2,128)(2,1)} reshape(bf16[64,32768]{1,0:T(8,128)(2,1)} %convolution_convert_fusion.1) | data formatting | bytes 8388608 | tf_op jit(solution)/shard_map/reshape | solution.py:40
  100.6 10.5 %all-to-all-start.1 = ((bf16[32,2,32768]{2,1,0:T(2,128)(2,1)}), bf16[32,2,32768]{2,1,0:T(2,128)(2,1)}, u32[]{:S(2)}, u32[]{:S(2)}) async-start(bf16[32,2,32768]{2,1,0:T(2,128)(2,1)} %reshape.74), calls=%async_computation.2 | async-start | bytes 8388608 | tf_op jit(solution)/shard_map/all_to_all | solution.py:44
  111.2 0.5 broadcast.49
  111.7 0.7 reduce.3
  112.4 0.1 eq.63
  112.5 96.4 %all-to-all-done.1 = bf16[32,2,32768]{2,1,0:T(2,128)(2,1)} async-done(((bf16[32,2,32768]{2,1,0:T(2,128)(2,1)}), bf16[32,2,32768]{2,1,0:T(2,128)(2,1)}, u32[]{:S(2)}, u32[]{:S(2)}) %all-to-all-start.1) | async-done | bytes 4194336 | tf_op jit(solution)/shard_map/all_to_all | solution.py:44
  208.9 7.3 %reshape.75 = bf16[64,32768]{1,0:T(8,128)(2,1)} reshape(bf16[32,2,32768]{2,1,0:T(2,128)(2,1)} %all-to-all-done.1) | data formatting | bytes 8388608 | tf_op jit(solution)/shard_map/reshape | solution.py:47
  216.2 2.9 fusion.6
  219.1 0.4 reshape.76
  219.5 1.1 divide_convert_fusion
  220.6 0.2 reshape.77
  220.8 3.2 convolution_convert_fusion
  224.0 7.6 %reshape.78 = bf16[32,2,32768]{2,1,0:T(2,128)(2,1)} reshape(bf16[64,32768]{1,0:T(8,128)(2,1)} %convolution_convert_fusion) | data formatting | bytes 8388608 | tf_op jit(solution)/shard_map/reshape | solution.py:62
  231.7 8.5 %all-to-all-start.2 = ((bf16[32,2,32768]{2,1,0:T(2,128)(2,1)}), bf16[32,2,32768]{2,1,0:T(2,128)(2,1)}, u32[]{:S(2)}, u32[]{:S(2)}) async-start(bf16[32,2,32768]{2,1,0:T(2,128)(2,1)} %reshape.78), calls=%async_computation.3 | async-start | bytes 8388608 | tf_op jit(solution)/shard_map/all_to_all | solution.py:63
  240.2 0.0 all-gather.2.cloned.1.call-start
  240.2 0.1 copy.38
  240.3 0.1 eq.67
  240.4 95.7 %all-to-all-done.2 = bf16[32,2,32768]{2,1,0:T(2,128)(2,1)} async-done(((bf16[32,2,32768]{2,1,0:T(2,128)(2,1)}), bf16[32,2,32768]{2,1,0:T(2,128)(2,1)}, u32[]{:S(2)}, u32[]{:S(2)}) %all-to-all-start.2) | async-done | bytes 4194336 | tf_op jit(solution)/shard_map/all_to_all | solution.py:63
  336.1 7.3 %reshape.79 = bf16[64,32768]{1,0:T(8,128)(2,1)} reshape(bf16[32,2,32768]{2,1,0:T(2,128)(2,1)} %all-to-all-done.2) | data formatting | bytes 8388608 | tf_op jit(solution)/shard_map/reshape | solution.py:63
  343.4 3.1 convolution_convert_fusion.2
  346.5 0.5 copy.48
  347.0 8.1 %fusion = f32[32,256,4,128]{3,1,2,0:T(8,128)} fusion(bf16[32,4,128,128]{3,2,1,0:T(8,128)(2,1)S(1)} %copy-done.1, bf16[32,128,256]{2,1,0:T(8,128)(2,1)S(1)} %bitcast.52), kind=kOutput, calls=%fused_computation.5 | convolution fusion | flops 1073741824 | bytes 23068672 | tf_op jit(solution)/shard_map/skij,sih->skjh/dot_general | solution.py:70
  355.1 17.7 %copy.40 = f32[128,128,256]{2,0,1:T(8,128)} copy(f32[128,128,256]{1,2,0:T(8,128)} %bitcast.47) | data formatting | bytes 33554432 | tf_op jit(solution)/shard_map/reshape | solution.py:74
  372.8 9.0 %convolution_convert_fusion.3 = bf16[4,128,256]{2,0,1:T(4,128)(2,1)S(1)} fusion(f32[128,128,256]{2,0,1:T(8,128)} %copy.40, s32[128]{0:T(128)S(1)} %eq.67), kind=kOutput, calls=%fused_computation.8 | convolution fusion | flops 201458176 | bytes 17039872 | tf_op jit(solution)/shard_map/bn,njh->bjh/dot_general | solution.py:75
  381.8 0.8 pad_maximum_fusion
  382.7 0.0 all-reduce.2.cloned.1.call-start
  382.7 30.2 %all-gather.2.cloned.1.call-done = bf16[4096,512]{1,0:T(8,128)(2,1)} async-done(((bf16[512,512]{1,0:T(8,128)(2,1)}), bf16[4096,512]{1,0:T(8,128)(2,1)}) %all-gather.2.cloned.1.call-update) | async-done | bytes 4194320 | tf_op jit(solution)/shard_map/all_gather | solution.py:82
  413.0 4.2 convolution_bitcast_fusion
  417.2 145.3 %all-reduce.2.cloned.1.call-done = f32[128,512]{0,1:T(8,128)} async-done(((f32[128,512]{0,1:T(8,128)}), f32[128,512]{0,1:T(8,128)}) %all-reduce.2.cloned.1.call-update) | async-done | bytes 262160 | tf_op jit(solution)/shard_map/psum | solution.py:86
  562.5 1.8 copy.42
  (28 shorter events, 0.2 us)
Async XLA Ops:
  7.2 1.2 copy-start
  7.2 62.4 %reduce-scatter.2.cloned.1.call-start = ((), (), s32[]{:S(2)}) async-start(), calls=%async_computation.4 | async-start | bytes 9437184 | tf_op jit(solution)/shard_map/reduce_scatter | solution.py:17
  13.8 0.7 copy-start.6
  13.8 1.0 copy-start.8
  13.8 13.3 %copy-start.5 = (s32[32,4]{0,1:T(4,128)S(1)}, s32[32,4]{0,1:T(4,128)}, u32[]{:S(2)}) copy-start(s32[32,4]{0,1:T(4,128)} %param.13) | copy-start | bytes 1540
  15.6 85.1 %all-to-all-start = ((s32[32,1,2]{2,1,0:T(1,128)}), s32[32,1,2]{2,1,0:T(1,128)S(1)}, u32[]{:S(2)}, u32[]{:S(2)}) async-start(s32[32,1,2]{2,1,0:T(1,128)} %bitcast.2), calls=%async_computation | async-start | bytes 32768 | tf_op jit(solution)/shard_map/all_to_all | solution.py:45
  70.8 0.8 copy-start.2
  100.6 10.5 %copy-start.7 = (s32[512]{0:T(512)S(1)}, s32[512]{0:T(512)}, u32[]{:S(2)}) copy-start(s32[512]{0:T(512)} %param.14) | copy-start | bytes 6148
  100.6 108.3 %all-to-all-start.1 = ((bf16[32,2,32768]{2,1,0:T(2,128)(2,1)}), bf16[32,2,32768]{2,1,0:T(2,128)(2,1)}, u32[]{:S(2)}, u32[]{:S(2)}) async-start(bf16[32,2,32768]{2,1,0:T(2,128)(2,1)} %reshape.74), calls=%async_computation.2 | async-start | bytes 8388608 | tf_op jit(solution)/shard_map/all_to_all | solution.py:44
  216.2 3.3 copy-start.3
  216.2 3.3 copy-start.4
  231.7 104.5 %all-to-all-start.2 = ((bf16[32,2,32768]{2,1,0:T(2,128)(2,1)}), bf16[32,2,32768]{2,1,0:T(2,128)(2,1)}, u32[]{:S(2)}, u32[]{:S(2)}) async-start(bf16[32,2,32768]{2,1,0:T(2,128)(2,1)} %reshape.78), calls=%async_computation.3 | async-start | bytes 8388608 | tf_op jit(solution)/shard_map/all_to_all | solution.py:63
  240.2 172.8 %all-gather.2.cloned.1.call-start = ((), (), s32[]{:S(2)}) async-start(), calls=%async_computation.5 | async-start | bytes 4718592 | tf_op jit(solution)/shard_map/all_gather | solution.py:82
  343.4 3.6 copy-start.1
  382.7 179.8 %all-reduce.2.cloned.1.call-start = ((), (), s32[]{:S(2)}) async-start(), calls=%async_computation.6 | async-start | bytes 524288 | tf_op jit(solution)/shard_map/psum | solution.py:86
Sparse Core Ops, SparseCore 0:
  13.9 55.5 reduce-scatter.1
  382.8 30.1 all-gather.1
  417.3 145.1 all-reduce.1
where the time goes:
time: 572 us; the launch traced here: 571 us
  waiting for transfers between devices  410 us (72%)
  local copies, waits for them, and re-layouts  64.1 us (11%)
  matrix products  47.8 us (8%)
  starting transfers between devices  30.6 us (5%)
  between operations  13.9 us (2%)
    psum x1, waiting for transfers between devices, local(): weight_grad = lax.psum(partial_grad, 'dom')  145 us
    all_to_all x1, waiting for transfers between devices, local(): lax.all_to_all(outgoing, 'dom', split_axis=0, concat_axis=0, tiled=True)  96.4 us
    all_to_all x1, waiting for transfers between devices, local(): lax.all_to_all(sending_back, 'dom', split_axis=0, concat_axis=0, tiled=True)  95.7 us
    reduce_scatter x1, waiting for transfers between devices, local(): lax.psum_scatter(jnp.dot(feats, projection, preferred_element_type=jnp.fl...  42.2 us
    all_gather x1, waiting for transfers between devices, local(): lax.all_gather(grad_proj, 'feat', axis=0, tiled=True)  30.2 us
    reshape x1, local copies, waits for them, and re-layouts, local(): products.reshape(slot_count * per_slot, tile_size, out_width)  17.7 us
    all_to_all x1, starting transfers between devices, local(): lax.all_to_all(labels, 'dom', split_axis=0, concat_axis=0, tiled=True)  11.5 us
  transfers between devices with their start and end apart: 6, of which 5 were waited for; matrix products, arithmetic and copies ran while one was open for 6% of the time, Pallas kernels for 0%

commit v1 on v0

--- a/solution.py
+++ b/solution.py
@@ -83,7 +83,7 @@
         (((0,), (0,)), ((), ())),
         preferred_element_type=jnp.float32,
     )
-    weight_grad = lax.psum(partial_grad, "dom")
+    weight_grad = jnp.sum(lax.all_gather(partial_grad, "dom"), axis=0)
     return (activated, weight_grad)
 
 

time: 572 us -> 537 us (0.939)
  waiting for transfers between devices: 410 us -> 369 us
    psum x1 -> x0, waiting for transfers between devices: 145 us -> none  [local(): weight_grad = lax.psum(partial_grad, 'dom')]
    all_gather x0 -> x1, waiting for transfers between devices: none -> 105 us  [local(): weight_grad = jnp.sum(lax.all_gather(partial_grad, 'dom'), axis=0)]
    unnamed x22 -> x23, local copies, waits for them, and re-layouts: 7.92 us -> 12.2 us
where the time goes in v1:
time: 537 us; the launch traced here: 536 us
  waiting for transfers between devices  369 us (69%)
  local copies, waits for them, and re-layouts  68.4 us (13%)
  matrix products  47.8 us (9%)
  starting transfers between devices  30.9 us (6%)
  between operations  13.9 us (3%)
  other arithmetic  5.89 us (1%)
    all_gather x1, waiting for transfers between devices, local(): weight_grad = jnp.sum(lax.all_gather(partial_grad, 'dom'), axis=0)  105 us
    all_to_all x1, waiting for transfers between devices, local(): lax.all_to_all(outgoing, 'dom', split_axis=0, concat_axis=0, tiled=True)  96.4 us
    all_to_all x1, waiting for transfers between devices, local(): lax.all_to_all(sending_back, 'dom', split_axis=0, concat_axis=0, tiled=True)  95.7 us
    reduce_scatter x1, waiting for transfers between devices, local(): lax.psum_scatter(jnp.dot(feats, projection, preferred_element_type=jnp.fl...  42.2 us
    all_gather x1, waiting for transfers between devices, local(): lax.all_gather(grad_proj, 'feat', axis=0, tiled=True)  30 us
    reshape x1, local copies, waits for them, and re-layouts, local(): products.reshape(slot_count * per_slot, tile_size, out_width)  17.7 us
    unnamed x23, local copies, waits for them, and re-layouts  12.2 us
    all_to_all x1, starting transfers between devices, local(): lax.all_to_all(labels, 'dom', split_axis=0, concat_axis=0, tiled=True)  11.5 us
  transfers between devices with their start and end apart: 6, of which 5 were waited for; matrix products, arithmetic and copies ran while one was open for 6% of the time, Pallas kernels for 0%

profile of v1, /device:TPU:2, one launch (start us, length us, event | category | flops | bytes accessed | tf_op | source)
XLA Modules:
  0.0 536.1 jit_solution(17545473035359634805)
XLA Ops:
  7.2 1.2 copy-done
  8.4 5.4 %fusion.12 = f32[4096,512]{1,0:T(8,128)} fusion(bf16[4096,128]{1,0:T(8,128)(2,1)S(1)} %copy-done, bf16[128,512]{1,0:T(8,128)(2,1)} %param.9), kind=kOutput, calls=%fused_computation.36 | convolution fusion | flops 536870912 | bytes 9568256 | tf_op jit(solution)/shard_map/dot_general | solution.py:18
  13.8 0.6 copy-done.6
  14.4 0.1 fusion.3
  14.6 0.2 select_reduce_fusion.1
  14.8 0.1 select_reduce_fusion
  14.9 0.7 sub.14
  15.6 11.5 %all-to-all-start = ((s32[32,1,2]{2,1,0:T(1,128)}), s32[32,1,2]{2,1,0:T(1,128)S(1)}, u32[]{:S(2)}, u32[]{:S(2)}) async-start(s32[32,1,2]{2,1,0:T(1,128)} %bitcast.2), calls=%async_computation | async-start | bytes 32768 | tf_op jit(solution)/shard_map/all_to_all | solution.py:45
  27.1 0.1 copy.33
  27.2 0.1 reshape.85
  27.3 42.2 %reduce-scatter.2.cloned.1.call-done = f32[512,512]{1,0:T(8,128)} async-done(((f32[4096,512]{1,0:T(8,128)}), f32[512,512]{1,0:T(8,128)}) %reduce-scatter.2.cloned.1.call-update) | async-done | bytes 1048592 | tf_op jit(solution)/shard_map/reduce_scatter | solution.py:17
  69.5 1.3 convert_element_type.48
  70.8 0.8 copy-done.2
  71.7 6.5 %gather_fusion = bf16[128,128,256]{2,1,0:T(8,128)(2,1)} fusion(bf16[4,128,256]{2,1,0:T(8,128)(2,1)S(1)} %bitcast.51, s32[1024]{0:T(1024)S(1)} %pad_clamp_fusion), kind=kCustom, calls=%fused_computation | custom fusion | bytes 16777728 | tf_op jit(solution)/shard_map/gather | solution.py:25
  78.2 7.0 %fusion.2 = bf16[32,128,256]{1,2,0:T(8,128)(2,1)S(1)} fusion(bf16[32,4,128,256]{3,2,1,0:T(8,128)(2,1)} %bitcast.53, bf16[32,4,128,128]{3,2,1,0:T(8,128)(2,1)} %param.10), kind=kOutput, calls=%fused_computation.8 | convolution fusion | flops 1074790400 | bytes 14680064 | tf_op jit(solution)/shard_map/skij,skjh->sih/dot_general | solution.py:26
  85.2 2.9 copy.45
  88.1 4.9 convolution_convert_fusion.1
  93.0 7.6 %reshape.74 = bf16[32,2,32768]{2,1,0:T(2,128)(2,1)} reshape(bf16[64,32768]{1,0:T(8,128)(2,1)} %convolution_convert_fusion.1) | data formatting | bytes 8388608 | tf_op jit(solution)/shard_map/reshape | solution.py:40
  100.6 10.5 %all-to-all-start.1 = ((bf16[32,2,32768]{2,1,0:T(2,128)(2,1)}), bf16[32,2,32768]{2,1,0:T(2,128)(2,1)}, u32[]{:S(2)}, u32[]{:S(2)}) async-start(bf16[32,2,32768]{2,1,0:T(2,128)(2,1)} %reshape.74), calls=%async_computation.2 | async-start | bytes 8388608 | tf_op jit(solution)/shard_map/all_to_all | solution.py:44
  111.2 0.5 broadcast.49
  111.7 0.7 reduce.3
  112.4 0.1 eq.63
  112.5 96.4 %all-to-all-done.1 = bf16[32,2,32768]{2,1,0:T(2,128)(2,1)} async-done(((bf16[32,2,32768]{2,1,0:T(2,128)(2,1)}), bf16[32,2,32768]{2,1,0:T(2,128)(2,1)}, u32[]{:S(2)}, u32[]{:S(2)}) %all-to-all-start.1) | async-done | bytes 4194336 | tf_op jit(solution)/shard_map/all_to_all | solution.py:44
  208.9 7.3 %reshape.75 = bf16[64,32768]{1,0:T(8,128)(2,1)} reshape(bf16[32,2,32768]{2,1,0:T(2,128)(2,1)} %all-to-all-done.1) | data formatting | bytes 8388608 | tf_op jit(solution)/shard_map/reshape | solution.py:47
  216.2 2.9 fusion.6
  219.1 0.4 reshape.76
  219.5 1.1 divide_convert_fusion
  220.6 0.2 reshape.77
  220.8 3.2 convolution_convert_fusion
  224.0 7.6 %reshape.78 = bf16[32,2,32768]{2,1,0:T(2,128)(2,1)} reshape(bf16[64,32768]{1,0:T(8,128)(2,1)} %convolution_convert_fusion) | data formatting | bytes 8388608 | tf_op jit(solution)/shard_map/reshape | solution.py:62
  231.7 8.5 %all-to-all-start.2 = ((bf16[32,2,32768]{2,1,0:T(2,128)(2,1)}), bf16[32,2,32768]{2,1,0:T(2,128)(2,1)}, u32[]{:S(2)}, u32[]{:S(2)}) async-start(bf16[32,2,32768]{2,1,0:T(2,128)(2,1)} %reshape.78), calls=%async_computation.3 | async-start | bytes 8388608 | tf_op jit(solution)/shard_map/all_to_all | solution.py:63
  240.2 0.1 copy.36
  240.3 0.1 eq.67
  240.4 95.7 %all-to-all-done.2 = bf16[32,2,32768]{2,1,0:T(2,128)(2,1)} async-done(((bf16[32,2,32768]{2,1,0:T(2,128)(2,1)}), bf16[32,2,32768]{2,1,0:T(2,128)(2,1)}, u32[]{:S(2)}, u32[]{:S(2)}) %all-to-all-start.2) | async-done | bytes 4194336 | tf_op jit(solution)/shard_map/all_to_all | solution.py:63
  336.1 7.3 %reshape.79 = bf16[64,32768]{1,0:T(8,128)(2,1)} reshape(bf16[32,2,32768]{2,1,0:T(2,128)(2,1)} %all-to-all-done.2) | data formatting | bytes 8388608 | tf_op jit(solution)/shard_map/reshape | solution.py:63
  343.4 3.1 convolution_convert_fusion.2
  346.5 0.5 copy.46
  347.0 8.1 %fusion = f32[32,256,4,128]{3,1,2,0:T(8,128)} fusion(bf16[32,4,128,128]{3,2,1,0:T(8,128)(2,1)S(1)} %copy-done.1, bf16[32,128,256]{2,1,0:T(8,128)(2,1)S(1)} %bitcast.58), kind=kOutput, calls=%fused_computation.6 | convolution fusion | flops 1073741824 | bytes 23068672 | tf_op jit(solution)/shard_map/skij,sih->skjh/dot_general | solution.py:70
  355.1 17.7 %copy.38 = f32[128,128,256]{2,0,1:T(8,128)} copy(f32[128,128,256]{1,2,0:T(8,128)} %bitcast.52) | data formatting | bytes 33554432 | tf_op jit(solution)/shard_map/reshape | solution.py:74
  372.8 9.0 %convolution_convert_fusion.3 = bf16[4,128,256]{2,0,1:T(4,128)(2,1)S(1)} fusion(f32[128,128,256]{2,0,1:T(8,128)} %copy.38, s32[128]{0:T(128)S(1)} %eq.67), kind=kOutput, calls=%fused_computation.9 | convolution fusion | flops 201458176 | bytes 17039872 | tf_op jit(solution)/shard_map/bn,njh->bjh/dot_general | solution.py:75
  381.8 0.8 pad_maximum_fusion
  382.7 0.3 all-gather.6.cloned.1.call-start
  383.0 30.0 %all-gather.4.cloned.1.call-done = bf16[4096,512]{1,0:T(8,128)(2,1)} async-done(((bf16[512,512]{1,0:T(8,128)(2,1)}), bf16[4096,512]{1,0:T(8,128)(2,1)}) %all-gather.4.cloned.1.call-update) | async-done | bytes 4194320 | tf_op jit(solution)/shard_map/all_gather | solution.py:82
  413.0 4.2 convolution_bitcast_fusion
  417.2 104.8 %all-gather.6.cloned.1.call-done = f32[4096,512]{0,1:T(8,128)} async-done(((f32[128,512]{0,1:T(8,128)}), f32[4096,512]{0,1:T(8,128)}) %all-gather.6.cloned.1.call-update) | async-done | bytes 8388624 | tf_op jit(solution)/shard_map/all_gather | solution.py:86
  522.0 5.2 copy.47
  527.2 1.6 bitcast_reduce_fusion
  528.8 0.8 copy.40
  (30 shorter events, 0.3 us)
Async XLA Ops:
  7.2 1.2 copy-start
  7.2 62.4 %reduce-scatter.2.cloned.1.call-start = ((), (), s32[]{:S(2)}) async-start(), calls=%async_computation.4 | async-start | bytes 9437184 | tf_op jit(solution)/shard_map/reduce_scatter | solution.py:17
  13.8 0.7 copy-start.6
  13.8 1.0 copy-start.8
  13.8 13.3 %copy-start.5 = (s32[32,4]{0,1:T(4,128)S(1)}, s32[32,4]{0,1:T(4,128)}, u32[]{:S(2)}) copy-start(s32[32,4]{0,1:T(4,128)} %param.13) | copy-start | bytes 1540
  15.6 85.1 %all-to-all-start = ((s32[32,1,2]{2,1,0:T(1,128)}), s32[32,1,2]{2,1,0:T(1,128)S(1)}, u32[]{:S(2)}, u32[]{:S(2)}) async-start(s32[32,1,2]{2,1,0:T(1,128)} %bitcast.2), calls=%async_computation | async-start | bytes 32768 | tf_op jit(solution)/shard_map/all_to_all | solution.py:45
  70.8 0.8 copy-start.2
  100.6 10.5 %copy-start.7 = (s32[512]{0:T(512)S(1)}, s32[512]{0:T(512)}, u32[]{:S(2)}) copy-start(s32[512]{0:T(512)} %param.14) | copy-start | bytes 6148
  100.6 108.3 %all-to-all-start.1 = ((bf16[32,2,32768]{2,1,0:T(2,128)(2,1)}), bf16[32,2,32768]{2,1,0:T(2,128)(2,1)}, u32[]{:S(2)}, u32[]{:S(2)}) async-start(bf16[32,2,32768]{2,1,0:T(2,128)(2,1)} %reshape.74), calls=%async_computation.2 | async-start | bytes 8388608 | tf_op jit(solution)/shard_map/all_to_all | solution.py:44
  216.2 3.3 copy-start.3
  216.2 3.3 copy-start.4
  231.7 104.5 %all-to-all-start.2 = ((bf16[32,2,32768]{2,1,0:T(2,128)(2,1)}), bf16[32,2,32768]{2,1,0:T(2,128)(2,1)}, u32[]{:S(2)}, u32[]{:S(2)}) async-start(bf16[32,2,32768]{2,1,0:T(2,128)(2,1)} %reshape.78), calls=%async_computation.3 | async-start | bytes 8388608 | tf_op jit(solution)/shard_map/all_to_all | solution.py:63
  240.2 172.8 %all-gather.4.cloned.1.call-start = ((), (), s32[]{:S(2)}) async-start(), calls=%async_computation.5 | async-start | bytes 4718592 | tf_op jit(solution)/shard_map/all_gather | solution.py:82
  343.4 3.6 copy-start.1
  382.7 139.3 %all-gather.6.cloned.1.call-start = ((), (), s32[]{:S(2)}) async-start(), calls=%async_computation.6 | async-start | bytes 8650752 | tf_op jit(solution)/shard_map/all_gather | solution.py:86
Sparse Core Ops, SparseCore 0:
  13.9 55.5 reduce-scatter.1
  382.8 30.1 all-gather.3
  417.3 104.6 all-gather.5
